TPU v7x, 32 devices: a whole 2x2x4 slice. The times are simulated.
32 devices in a mesh: section: 2 (over x), space: 16 (over z, y, core).
Axes of the slice: x: 2, y: 2, z: 4, core: 2. Of those that a mesh axis runs over, the one named last changes fastest.
Arguments:
- input_tiles: bfloat16 [16, 2, 4, 8, 8, 256], P('space'), may hold values from -6 to 6
- saved_tiles: bfloat16 [16, 2, 32, 4, 4, 128], P('space'), may hold values from -6 to 6
- out_grad_tiles: bfloat16 [16, 2, 64, 2, 2, 64], P('space'), may hold values from -1 to 1
- kernel_first: bfloat16 [32, 4, 3, 3, 3], replicated, may hold values from -0.625 to 0.625
- bias_first: float32 [32], replicated, may hold values from -3 to 3
- kernel_second: bfloat16 [64, 32, 3, 3, 3], replicated, may hold values from -0.21875 to 0.21875
- bias_second: float32 [64], replicated, may hold values from -3 to 3
Outputs:
- grad_kernel_first: float32 [32, 4, 3, 3, 3], replicated
- grad_bias_first: float32 [32], replicated
- grad_kernel_second: float32 [64, 32, 3, 3, 3], replicated
- grad_bias_second: float32 [64], replicated
All inputs are finite; a program needn't handle non-finite values.
Results may differ from a plain program's by a relative error of at most 0.0031.
Values may be sent and summed in bfloat16 or wider, within the bound.
No kernel may reach another device: no remote copies, remote signals or barrier semaphores. Data moves between devices by JAX's collectives and lax.ppermute only.
A program may use at most 128 MiB of HBM per device.

v0:
```python
import jax
import jax.numpy as jnp
from jax import lax
from jax.sharding import PartitionSpec as P

GY = 8


def from_behind(value, axis, steps):
    count = lax.axis_size(axis)
    first, last = (max(0, -steps), min(count, count - steps))
    return lax.ppermute(value, axis, [(source, source + steps) for source in range(first, last)])


def correlate(padded, kernel):
    return lax.conv_general_dilated(
        padded,
        kernel,
        (1, 1, 1),
        "VALID",
        dimension_numbers=("NCDHW", "OIDHW", "NCDHW"),
        preferred_element_type=jnp.float32,
    )


def kernel_grad(padded, grads):
    result = lax.conv_general_dilated(
        padded,
        grads,
        (1, 1, 1),
        "VALID",
        dimension_numbers=("CNDHW", "IODHW", "NCDHW"),
        preferred_element_type=jnp.float32,
    )
    return jnp.transpose(result, (1, 0, 2, 3, 4))


def flipped(kernel):
    return jnp.transpose(kernel[:, :, ::-1, ::-1, ::-1], (1, 0, 2, 3, 4))


def spread_up(grad):
    batch, channels, rows_y, rows_z, rows_x = grad.shape
    value = grad.astype(jnp.float32) * 0.125
    value = jnp.broadcast_to(
        value[:, :, :, None, :, None, :, None], (batch, channels, rows_y, 2, rows_z, 2, rows_x, 2)
    )
    return value.reshape(batch, channels, 2 * rows_y, 2 * rows_z, 2 * rows_x)


def slope(pre):
    return jnp.where(pre > 0, 1.0, 0.3)


def bias_column(bias):
    return bias[None, :, None, None, None]


def widen_last(field):
    return jnp.pad(field, ((0, 0), (0, 0), (0, 0), (0, 0), (1, 1)))


def extend(field):
    grid_z = lax.axis_size("space") // GY
    place = lax.axis_index("space") % grid_z
    last_plane = field[:, :, :, -1:]
    first_plane = field[:, :, :, :1]
    last_plane = jnp.where(place < grid_z - 1, last_plane, jnp.zeros_like(last_plane))
    first_plane = jnp.where(place > 0, first_plane, jnp.zeros_like(first_plane))
    low_z = from_behind(last_plane, "space", 1)
    high_z = from_behind(first_plane, "space", -1)
    wide = jnp.concatenate([low_z, field, high_z], axis=3)
    low_y = from_behind(wide[:, :, -1:], "space", grid_z)
    high_y = from_behind(wide[:, :, :1], "space", -grid_z)
    return widen_last(jnp.concatenate([low_y, wide, high_y], axis=2))


def second_delta(second_ext, cotangent, kernel_second, bias_second):
    pre_two = correlate(second_ext, kernel_second) + bias_column(bias_second)
    return (spread_up(cotangent) * slope(pre_two)).astype(jnp.bfloat16)


def first_grads(first_ext, arrived, kernel_first, bias_first):
    pre_one = correlate(first_ext, kernel_first) + bias_column(bias_first)
    delta_one = (spread_up(arrived) * slope(pre_one)).astype(jnp.bfloat16)
    return (
        kernel_grad(first_ext, delta_one),
        jnp.sum(delta_one, axis=(0, 2, 3, 4), dtype=jnp.float32),
    )


def on_device(
    input_tiles, saved_tiles, out_grad_tiles, kernel_first, bias_first, kernel_second, bias_second
):
    first = input_tiles[0]
    second = saved_tiles[0]
    cotangent = out_grad_tiles[0]
    section = lax.axis_index("section")
    batches = first.shape[0]
    flipped_two = flipped(kernel_second)
    share = batches // lax.axis_size("section")
    offset = section * share
    local_first = lax.dynamic_slice_in_dim(first, offset, share, 0)
    local_second = lax.dynamic_slice_in_dim(second, offset, share, 0)
    local_cot = lax.dynamic_slice_in_dim(cotangent, offset, share, 0)
    second_ext = extend(local_second)
    first_ext = extend(local_first)
    delta_two = second_delta(second_ext, local_cot, kernel_second, bias_second)
    delta_ext = extend(delta_two)
    grad_w_two = kernel_grad(second_ext, delta_two)
    grad_b_two = jnp.sum(delta_two, axis=(0, 2, 3, 4), dtype=jnp.float32)
    back = correlate(delta_ext, flipped_two).astype(jnp.bfloat16)
    grad_w_one, grad_b_one = first_grads(first_ext, back, kernel_first, bias_first)
    total = lax.psum((grad_w_one, grad_b_one, grad_w_two, grad_b_two), ("section", "space"))
    return (total[0], total[1], total[2], total[3])


def solution(mesh):
    placed = (
        P("space", None, None, None, None, None),
        P("space", None, None, None, None, None),
        P("space", None, None, None, None, None),
        P(),
        P(),
        P(),
        P(),
    )
    return jax.shard_map(
        on_device, mesh=mesh, in_specs=placed, out_specs=(P(), P(), P(), P()), check_vma=False
    )
```

profile of v0, /device:TPU:0, one launch (start us, length us, event | category | flops | bytes accessed | tf_op | source)
XLA Modules:
  0.0 405.5 jit_solution(2935043332899590350)
XLA Ops:
  8.2 2.4 collective-permute-start
  13.0 5.2 %collective-permute-start.4 = (bf16[1,32,4,1,128]{4,1,3,2,0:T(8,128)(2,1)S(1)}, bf16[1,32,4,1,128]{4,1,3,2,0:T(8,128)(2,1)S(1)}, u32[]{:S(2)}, u32[]{:S(2)}) collective-permute-start(bf16[1,32,4,1,128]{4,1,3,2,0:T(8,128)(2,1)S(1)} %get-tuple-element.19), channel_id=1, source_target_pairs={{0,1},{1,2},{2,3},{3,4},{4,5},{5,6},{6,7},{7,8},{8,9},{9,10},{10,1... | collective-permute-start | bytes 98312 | tf_op jit(solution)/shard_map/ppermute | solution.py:12
  20.3 9.1 %copy.94 = bf16[1,4,8,8,256]{1,0,4,3,2:T(2,128)(2,1)} copy(bf16[1,4,8,8,256]{4,3,2,1,0:T(8,128)(2,1)S(1)} %dynamic-slice_bitcast_fusion) | data formatting | bytes 262144 | tf_op jit(solution)/shard_map/dynamic_slice | solution.py:103
  30.8 7.0 %pad_maximum_fusion.3 = (bf16[1,4,1,10,256]{1,0,4,3,2:T(2,128)(2,1)}, bf16[1,4,1,10,256]{1,0,4,3,2:T(2,128)(2,1)}) fusion(bf16[1,4,8,1,256]{1,0,4,3,2:T(2,128)(2,1)S(1)} %copy.95, bf16[1,4,8,8,256]{1,0,4,3,2:T(2,128)(2,1)} %copy.94, bf16[1,4,8,1,256]{1,0,4,3,2:T(2,128)(2,1)S(1)} %copy.93), kind=kLoop, calls=%fused_computation.43 | loop fusion | flops 40960 | bytes 204800 | tf_op jit(solution)/shard_map/slice | solution.py:73
  37.9 2.5 copy.96
  40.4 5.9 %collective-permute-start.2 = (bf16[1,4,1,10,256]{4,1,3,2,0:T(4,128)(2,1)S(1)}, bf16[1,4,1,10,256]{4,1,3,2,0:T(4,128)(2,1)S(1)}, u32[]{:S(2)}, u32[]{:S(2)}) collective-permute-start(bf16[1,4,1,10,256]{4,1,3,2,0:T(4,128)(2,1)S(1)} %copy.96), channel_id=1, source_target_pairs={{0,2},{1,3},{2,4},{3,5},{4,6},{5,7},{6,8},{7,9},{8,10},{9,11},{10,... | collective-permute-start | bytes 61448 | tf_op jit(solution)/shard_map/ppermute | solution.py:12
  46.3 2.5 copy.97
  50.1 5.9 %collective-permute-start.6 = (bf16[1,32,1,6,128]{4,1,3,2,0:T(8,128)(2,1)S(1)}, bf16[1,32,1,6,128]{4,1,3,2,0:T(8,128)(2,1)S(1)}, u32[]{:S(2)}, u32[]{:S(2)}) collective-permute-start(bf16[1,32,1,6,128]{4,1,3,2,0:T(8,128)(2,1)S(1)} %get-tuple-element.17), channel_id=1, source_target_pairs={{0,2},{1,3},{2,4},{3,5},{4,6},{5,7},{6,8},{7,9},{8,10},{9,11},{10,... | collective-permute-start | bytes 147464 | tf_op jit(solution)/shard_map/ppermute | solution.py:12
  61.8 40.1 %pad_maximum_fusion = bf16[1,4,10,10,256]{1,0,4,3,2:T(2,128)(2,1)} fusion(bf16[1,4,1,10,256]{1,0,4,3,2:T(2,128)(2,1)} %copy.99, bf16[1,4,8,1,256]{1,0,4,3,2:T(2,128)(2,1)S(1)} %copy.95, bf16[1,4,8,8,256]{1,0,4,3,2:T(2,128)(2,1)} %copy.94, bf16[1,4,8,1,256]{1,0,4,3,2:T(2,128)(2,1)S(1)} %copy.93, bf16[1,4,1,10,256]{1,0,4,3,2:T(2,128)(2,1)} %copy.98), kind=kLoop, calls=%fused_computation | loop fusion | flops 409600 | bytes 409600 | tf_op jit(solution)/shard_map/concatenate | solution.py:75
  101.9 23.7 %copy.113 = bf16[1,4,10,10,256]{4,1,3,2,0:T(4,128)(2,1)S(1)} copy(bf16[1,4,10,10,256]{1,0,4,3,2:T(2,128)(2,1)} %pad_maximum_fusion) | data formatting | bytes 409600 | tf_op jit(solution)/shard_map/concatenate | solution.py:75
  126.6 4.3 %copy.115 = bf16[4,10,10,1,8,33]{4,0,5,2,1,3:T(4,128)(2,1)} copy(bf16[4,10,10,1,8,33]{5,4,0,2,1,3:T(8,128)(2,1)S(1)} %reshape.57) | data formatting | bytes 422400 | tf_op jit(solution)/shard_map/conv_general_dilated | solution.py:16
  132.1 20.5 %fusion = f32[8,8,8,33,32]{4,2,3,1,0:T(8,128)S(1)} fusion(f32[32]{0:T(128)S(1)} %copy-done.9, pred[8,33]{0,1:T(8,128)(4,1)S(1)} %copy-done.11, bf16[32,4,3,3,3]{0,1,4,3,2:T(4,128)(2,1)S(1)} %copy-done.8, bf16[4,10,10,1,7,2]{4,0,5,2,1,3:T(4,128)(2,1)S(1)} %slice.64, bf16[4,10,10,1,8,33]{4,0,5,2,1,3:T(4,128)(2,1)} %copy.115), kind=kOutput, calls=%fused_computation.2 | convolution fusion | flops 119619840 | bytes 2392392 | tf_op jit(solution)/shard_map/conv_general_dilated | solution.py:16
  152.6 6.0 %copy.121 = f32[8,8,8,33,32]{4,3,2,1,0:T(8,128)} copy(f32[8,8,8,33,32]{4,2,3,1,0:T(8,128)S(1)} %fusion) | data formatting | bytes 4325376 | tf_op jit(solution)/shard_map/jit(_where)/select_n | solution.py:52
  158.6 9.5 %reshape.76 = f32[8,8,1,264,32]{4,3,1,0,2:T(8,128)} reshape(f32[8,8,8,33,32]{4,3,2,1,0:T(8,128)} %copy.121) | data formatting | bytes 4325376 | tf_op jit(solution)/shard_map/jit(_where)/select_n | solution.py:52
  170.8 3.0 copy.103
  174.8 3.5 fusion.53
  185.7 4.7 %copy.119 = bf16[1,32,6,6,128]{1,0,4,3,2:T(2,128)(2,1)S(1)} copy(bf16[1,32,6,6,128]{4,1,3,2,0:T(8,128)(2,1)} %pad_maximum_fusion.4) | data formatting | bytes 589824 | tf_op jit(solution)/shard_map/concatenate | solution.py:75
  193.2 7.7 %collective-permute-start.10 = (bf16[1,64,1,6,128]{4,1,3,2,0:T(8,128)(2,1)}, bf16[1,64,1,6,128]{4,1,3,2,0:T(8,128)(2,1)S(1)}, u32[]{:S(2)}, u32[]{:S(2)}) collective-permute-start(bf16[1,64,1,6,128]{4,1,3,2,0:T(8,128)(2,1)} %get-tuple-element.15), channel_id=1, source_target_pairs={{0,2},{1,3},{2,4},{3,5},{4,6},{5,7},{6,8},{7,9},{8,10},{9,11},{10,... | collective-permute-start | bytes 294920 | tf_op jit(solution)/shard_map/ppermute | solution.py:12
  202.4 14.7 %fusion.58 = f32[64,32,3,3,3]{0,1,4,3,2:T(8,128)} fusion(bf16[1,32,6,6,128]{1,0,4,3,2:T(2,128)(2,1)S(1)} %copy.119, bf16[1,64,4,4,128]{1,3,4,2,0:T(4,128)(2,1)S(1)} %get-tuple-element.8), kind=kOutput, calls=%fused_computation.50 | convolution fusion | flops 225312768 | bytes 778240 | tf_op jit(solution)/shard_map/transpose | solution.py:35
  220.7 4.3 %fusion.50 = f32[4,4,8,17,32]{4,2,3,1,0:T(8,128)S(1)} fusion(bf16[64,32,3,3,3]{0,1,4,3,2:T(8,128)(2,1)S(1)} %copy-done.7, bf16[64,6,6,1,7,2]{0,4,5,2,1,3:T(8,128)(2,1)S(1)} %slice.62, bf16[64,6,6,1,8,17]{0,4,5,2,1,3:T(8,128)(2,1)S(1)} %copy.110, pred[8,17]{0,1:T(8,128)(4,1)S(1)} %copy-done.12), kind=kOutput, calls=%fused_computation.40 | convolution fusion | flops 243027968 | bytes 1080456 | tf_op jit(solution)/shard_map/conv_general_dilated | solution.py:16
  225.6 7.3 %broadcast_in_dim.41 = f32[32,4,2,4,2,128,2]{0,6,5,4,3,2,1:T(2,128)} broadcast(f32[32,4,4,128]{0,3,2,1:T(8,128)S(1)} %copy.112), dimensions={0,1,3,5} | broadcast | bytes 2359296 | tf_op jit(solution)/shard_map/broadcast_in_dim | solution.py:45
  232.9 7.6 %convert_reduce_fusion = (f32[32]{0:T(128)}, bf16[1,32,8,8,256]{1,4,3,2,0:T(8,128)(2,1)S(1)}) fusion(f32[1,32,8,8,256]{1,4,3,2,0:T(8,128)} %bitcast.76, f32[8,8,1,264,32]{4,3,1,0,2:T(8,128)} %reshape.76), kind=kLoop, calls=%fused_computation.6 | loop fusion | flops 2097120 | bytes 5243008 | tf_op jit(solution)/shard_map/reduce_sum | solution.py:88
  240.5 111.0 %fusion.3 = f32[32,4,3,3,3]{0,1,4,3,2:T(4,128)S(1)} fusion(bf16[1,4,10,10,256]{1,0,4,3,2:T(2,128)(2,1)} %pad_maximum_fusion, bf16[1,32,8,8,256]{1,4,3,2,0:T(8,128)(2,1)S(1)} %get-tuple-element.10), kind=kOutput, calls=%fused_computation.7 | convolution fusion | flops 112951296 | bytes 1267200 | tf_op jit(solution)/shard_map/transpose | solution.py:35
  351.5 44.9 %all-reduce = (f32[32,4,3,3,3]{0,1,4,3,2:T(4,128)}, f32[32]{0:T(128)}, f32[64]{0:T(128)}) all-reduce(f32[32,4,3,3,3]{0,1,4,3,2:T(4,128)S(1)} %fusion.3, f32[32]{0:T(128)S(1)} %copy-done.4, f32[64]{0:T(128)S(1)} %copy-done.5), channel_id=1, replica_groups=mesh['section'=2,'space'=16] {'section','space'}, use_global_device_ids=true, to_apply=%region_0.1 | all-reduce | flops 3552 | bytes 28416 | tf_op jit(solution)/shard_map/psum | solution.py:114
  (88 shorter events, 37.1 us)
Async XLA Ops:
  7.2 1.0 copy-start
  7.2 389.2 %all-reduce.3.cloned.1.call-start = ((), (), s32[]{:S(2)}) async-start(), calls=%async_computation | async-start | bytes 884736 | tf_op jit(solution)/shard_map/psum | solution.py:114
  8.2 21.3 %collective-permute-start = (bf16[1,4,8,1,256]{4,2,3,1,0:T(8,128)(2,1)S(1)}, bf16[1,4,8,1,256]{4,2,3,1,0:T(8,128)(2,1)S(1)}, u32[]{:S(2)}, u32[]{:S(2)}) collective-permute-start(bf16[1,4,8,1,256]{4,2,3,1,0:T(8,128)(2,1)S(1)} %copy.91), channel_id=1, source_target_pairs={{0,1},{1,2},{2,3},{3,4},{4,5},{5,6},{6,7},{7,8},{8,9},{9,10},{10,1... | collective-permute-start | bytes 49160 | tf_op jit(solution)/shard_map/ppermute | solution.py:12
  10.7 19.5 %collective-permute-start.1 = (bf16[1,4,8,1,256]{4,2,3,1,0:T(8,128)(2,1)S(1)}, bf16[1,4,8,1,256]{4,2,3,1,0:T(8,128)(2,1)S(1)}, u32[]{:S(2)}, u32[]{:S(2)}) collective-permute-start(bf16[1,4,8,1,256]{4,2,3,1,0:T(8,128)(2,1)S(1)} %copy.92), channel_id=1, source_target_pairs={{1,0},{2,1},{3,2},{4,3},{5,4},{6,5},{7,6},{8,7},{9,8},{10,9},{11,1... | collective-permute-start | bytes 49160 | tf_op jit(solution)/shard_map/ppermute | solution.py:12
  13.0 37.1 %collective-permute-start.4 = (bf16[1,32,4,1,128]{4,1,3,2,0:T(8,128)(2,1)S(1)}, bf16[1,32,4,1,128]{4,1,3,2,0:T(8,128)(2,1)S(1)}, u32[]{:S(2)}, u32[]{:S(2)}) collective-permute-start(bf16[1,32,4,1,128]{4,1,3,2,0:T(8,128)(2,1)S(1)} %get-tuple-element.19), channel_id=1, source_target_pairs={{0,1},{1,2},{2,3},{3,4},{4,5},{5,6},{6,7},{7,8},{8,9},{9,10},{10,1... | collective-permute-start | bytes 98312 | tf_op jit(solution)/shard_map/ppermute | solution.py:12
  18.1 32.0 %collective-permute-start.5 = (bf16[1,32,4,1,128]{4,1,3,2,0:T(8,128)(2,1)S(1)}, bf16[1,32,4,1,128]{4,1,3,2,0:T(8,128)(2,1)S(1)}, u32[]{:S(2)}, u32[]{:S(2)}) collective-permute-start(bf16[1,32,4,1,128]{4,1,3,2,0:T(8,128)(2,1)S(1)} %get-tuple-element.20), channel_id=1, source_target_pairs={{1,0},{2,1},{3,2},{4,3},{5,4},{6,5},{7,6},{8,7},{9,8},{10,9},{11,1... | collective-permute-start | bytes 98312 | tf_op jit(solution)/shard_map/ppermute | solution.py:12
  40.4 17.1 %collective-permute-start.2 = (bf16[1,4,1,10,256]{4,1,3,2,0:T(4,128)(2,1)S(1)}, bf16[1,4,1,10,256]{4,1,3,2,0:T(4,128)(2,1)S(1)}, u32[]{:S(2)}, u32[]{:S(2)}) collective-permute-start(bf16[1,4,1,10,256]{4,1,3,2,0:T(4,128)(2,1)S(1)} %copy.96), channel_id=1, source_target_pairs={{0,2},{1,3},{2,4},{3,5},{4,6},{5,7},{6,8},{7,9},{8,10},{9,11},{10,... | collective-permute-start | bytes 61448 | tf_op jit(solution)/shard_map/ppermute | solution.py:12
  48.8 10.9 %collective-permute-start.3 = (bf16[1,4,1,10,256]{4,1,3,2,0:T(4,128)(2,1)S(1)}, bf16[1,4,1,10,256]{4,1,3,2,0:T(4,128)(2,1)S(1)}, u32[]{:S(2)}, u32[]{:S(2)}) collective-permute-start(bf16[1,4,1,10,256]{4,1,3,2,0:T(4,128)(2,1)S(1)} %copy.97), channel_id=1, source_target_pairs={{2,0},{3,1},{4,2},{5,3},{6,4},{7,5},{8,6},{9,7},{10,8},{11,9},{12,... | collective-permute-start | bytes 61448 | tf_op jit(solution)/shard_map/ppermute | solution.py:12
  50.1 118.0 %collective-permute-start.6 = (bf16[1,32,1,6,128]{4,1,3,2,0:T(8,128)(2,1)S(1)}, bf16[1,32,1,6,128]{4,1,3,2,0:T(8,128)(2,1)S(1)}, u32[]{:S(2)}, u32[]{:S(2)}) collective-permute-start(bf16[1,32,1,6,128]{4,1,3,2,0:T(8,128)(2,1)S(1)} %get-tuple-element.17), channel_id=1, source_target_pairs={{0,2},{1,3},{2,4},{3,5},{4,6},{5,7},{6,8},{7,9},{8,10},{9,11},{10,... | collective-permute-start | bytes 147464 | tf_op jit(solution)/shard_map/ppermute | solution.py:12
  56.0 112.2 %collective-permute-start.7 = (bf16[1,32,1,6,128]{4,1,3,2,0:T(8,128)(2,1)S(1)}, bf16[1,32,1,6,128]{4,1,3,2,0:T(8,128)(2,1)S(1)}, u32[]{:S(2)}, u32[]{:S(2)}) collective-permute-start(bf16[1,32,1,6,128]{4,1,3,2,0:T(8,128)(2,1)S(1)} %get-tuple-element.18), channel_id=1, source_target_pairs={{2,0},{3,1},{4,2},{5,3},{6,4},{7,5},{8,6},{9,7},{10,8},{11,9},{12,... | collective-permute-start | bytes 147464 | tf_op jit(solution)/shard_map/ppermute | solution.py:12
  126.6 5.5 %copy-start.8 = (bf16[32,4,3,3,3]{0,1,4,3,2:T(4,128)(2,1)S(1)}, bf16[32,4,3,3,3]{0,1,4,3,2:T(4,128)(2,1)}, u32[]{:S(2)}) copy-start(bf16[32,4,3,3,3]{0,1,4,3,2:T(4,128)(2,1)} %param.10) | copy-start | bytes 20740
  126.6 5.5 %copy-start.9 = (f32[32]{0:T(128)S(1)}, f32[32]{0:T(128)}, u32[]{:S(2)}) copy-start(f32[32]{0:T(128)} %param.11) | copy-start | bytes 388
  126.6 5.5 %copy-start.11 = (pred[8,33]{0,1:T(8,128)(4,1)S(1)}, pred[8,33]{0,1:T(8,128)(4,1)}, u32[]{:S(2)}) copy-start(pred[8,33]{0,1:T(8,128)(4,1)} %constant.64) | copy-start | bytes 796
  170.8 4.0 copy-start.6
  170.8 4.0 copy-start.10
  170.8 4.0 copy-start.12
  178.9 6.1 %copy-start.3 = (bf16[1,32,1,6,128]{4,1,3,2,0:T(8,128)(2,1)S(1)}, bf16[1,32,1,6,128]{4,1,3,2,0:T(8,128)(2,1)}, u32[]{:S(2)}) copy-start(bf16[1,32,1,6,128]{4,1,3,2,0:T(8,128)(2,1)} %copy-done.2) | copy-start | bytes 147460
  181.6 8.8 %collective-permute-start.8 = (bf16[1,64,4,1,128]{1,3,4,2,0:T(2,128)(2,1)}, bf16[1,64,4,1,128]{1,3,4,2,0:T(2,128)(2,1)}, u32[]{:S(2)}, u32[]{:S(2)}) collective-permute-start(bf16[1,64,4,1,128]{1,3,4,2,0:T(2,128)(2,1)} %get-tuple-element.13), channel_id=1, source_target_pairs={{0,1},{1,2},{2,3},{3,4},{4,5},{5,6},{6,7},{7,8},{8,9},{9,10},{10,1... | collective-permute-start | bytes 196616 | tf_op jit(solution)/shard_map/ppermute | solution.py:12
  183.6 7.8 %collective-permute-start.9 = (bf16[1,64,4,1,128]{1,3,4,2,0:T(2,128)(2,1)}, bf16[1,64,4,1,128]{1,3,4,2,0:T(2,128)(2,1)}, u32[]{:S(2)}, u32[]{:S(2)}) collective-permute-start(bf16[1,64,4,1,128]{1,3,4,2,0:T(2,128)(2,1)} %get-tuple-element.14), channel_id=1, source_target_pairs={{1,0},{2,1},{3,2},{4,3},{5,4},{6,5},{7,6},{8,7},{9,8},{10,9},{11,1... | collective-permute-start | bytes 196616 | tf_op jit(solution)/shard_map/ppermute | solution.py:12
  193.2 24.0 %collective-permute-start.10 = (bf16[1,64,1,6,128]{4,1,3,2,0:T(8,128)(2,1)}, bf16[1,64,1,6,128]{4,1,3,2,0:T(8,128)(2,1)S(1)}, u32[]{:S(2)}, u32[]{:S(2)}) collective-permute-start(bf16[1,64,1,6,128]{4,1,3,2,0:T(8,128)(2,1)} %get-tuple-element.15), channel_id=1, source_target_pairs={{0,2},{1,3},{2,4},{3,5},{4,6},{5,7},{6,8},{7,9},{8,10},{9,11},{10,... | collective-permute-start | bytes 294920 | tf_op jit(solution)/shard_map/ppermute | solution.py:12
  201.0 16.2 %collective-permute-start.11 = (bf16[1,64,1,6,128]{4,1,3,2,0:T(8,128)(2,1)S(1)}, bf16[1,64,1,6,128]{4,1,3,2,0:T(8,128)(2,1)}, u32[]{:S(2)}, u32[]{:S(2)}) collective-permute-start(bf16[1,64,1,6,128]{4,1,3,2,0:T(8,128)(2,1)S(1)} %get-tuple-element.16), channel_id=1, source_target_pairs={{2,0},{3,1},{4,2},{5,3},{6,4},{7,5},{8,6},{9,7},{10,8},{11,9},{12,... | collective-permute-start | bytes 294920 | tf_op jit(solution)/shard_map/ppermute | solution.py:12
  240.5 111.0 %copy-start.4 = (f32[32]{0:T(128)S(1)}, f32[32]{0:T(128)}, u32[]{:S(2)}) copy-start(f32[32]{0:T(128)} %get-tuple-element.9) | copy-start | bytes 388
  240.5 111.0 %copy-start.5 = (f32[64]{0:T(128)S(1)}, f32[64]{0:T(128)}, u32[]{:S(2)}) copy-start(f32[64]{0:T(128)} %get-tuple-element.7) | copy-start | bytes 772
  240.5 157.7 %copy-start.1 = (bf16[1,2,4,8,8,256]{5,4,3,2,1,0:T(8,128)(2,1)S(1)}, bf16[1,2,4,8,8,256]{5,4,3,2,1,0:T(8,128)(2,1)}, u32[]{:S(2)}) copy-start(bf16[1,2,4,8,8,256]{5,4,3,2,1,0:T(8,128)(2,1)} %param.7) | copy-start | bytes 786436
  (2 other events, 1.6 us)
Sparse Core Ops, SparseCore 0:
  217.3 131.7 all-reduce.2
where the time goes:
time: 411 us; the launch traced here: 406 us
  matrix products  154 us (37%)
  local copies, waits for them, and re-layouts  93.5 us (23%)
  other arithmetic  60.7 us (15%)
  blocking collectives  44.9 us (11%)
  starting transfers between devices  37.2 us (9%)
  between operations  15.1 us (4%)
    transpose x2, matrix products, kernel_grad(): return jnp.transpose(result, (1, 0, 2, 3, 4))  126 us
    psum x1, blocking collectives, on_device(): lax.psum((grad_w_one, grad_b_one, grad_w_two, grad_b_two), ('section', 's...  44.9 us
    concatenate x4, other arithmetic, extend(): return widen_last(jnp.concatenate([low_y, wide, high_y], axis=2))  41.9 us
    ppermute x12, starting transfers between devices, from_behind(): lax.ppermute(value, axis, [(source, source + steps) for source in range(f...  37.2 us
    concatenate x5, local copies, waits for them, and re-layouts, extend(): return widen_last(jnp.concatenate([low_y, wide, high_y], axis=2))  29.2 us
    conv_general_dilated x3, matrix products, correlate(): lax.conv_general_dilated(padded, kernel, (1, 1, 1), 'VALID', dimension_nu...  28.4 us
    select_n x3, local copies, waits for them, and re-layouts, slope(): return jnp.where(pre > 0, 1.0, 0.3)  15.8 us
    conv_general_dilated x9, local copies, waits for them, and re-layouts, correlate(): lax.conv_general_dilated(padded, kernel, (1, 1, 1), 'VALID', dimension_nu...  12.5 us
  transfers between devices with their start and end apart: 13, of which 0 were waited for; matrix products, arithmetic and copies ran while one was open for 71% of the time, Pallas kernels for 0%

commit v1 on v0

--- a/solution.py
+++ b/solution.py
@@ -111,7 +111,8 @@
     grad_b_two = jnp.sum(delta_two, axis=(0, 2, 3, 4), dtype=jnp.float32)
     back = correlate(delta_ext, flipped_two).astype(jnp.bfloat16)
     grad_w_one, grad_b_one = first_grads(first_ext, back, kernel_first, bias_first)
-    total = lax.psum((grad_w_one, grad_b_one, grad_w_two, grad_b_two), ("section", "space"))
+    partial = lax.psum((grad_w_one, grad_b_one, grad_w_two, grad_b_two), "space")
+    total = lax.psum(partial, "section")
     return (total[0], total[1], total[2], total[3])
 
 

time: 411 us -> 490 us (1.19)
  waiting for transfers between devices: 0.05 us -> 50.5 us
  blocking collectives: 44.9 us -> 69.2 us
  matrix products: 154 us -> 163 us
    psum x1 -> x2, waiting for transfers between devices: 0.01 us -> 50.4 us  [the longest x1 50.4 us: on_device(): lax.psum((grad_w_one, grad_b_one, grad_w_two, grad_b_two), 'space')]
    psum x1 -> x2, blocking collectives: 44.9 us -> 69.2 us  [the longest x1 60 us: on_device(): lax.psum((grad_w_one, grad_b_one, grad_w_two, grad_b_two), 'space')]
    transpose x2, matrix products: 126 us -> 135 us  [kernel_grad(): return jnp.transpose(result, (1, 0, 2, 3, 4))]
  transfers between devices with their start and end apart: 13 -> 14, of which waited for: 0 -> 1; matrix products, arithmetic and copies ran while one was open for 71% -> 61% of each run, Pallas kernels for 0% -> 0%
where the time goes in v1:
time: 490 us; the launch traced here: 485 us
  matrix products  163 us (33%)
  local copies, waits for them, and re-layouts  91.7 us (19%)
  blocking collectives  69.2 us (14%)
  other arithmetic  58.5 us (12%)
  waiting for transfers between devices  50.5 us (10%)
  starting transfers between devices  37.1 us (8%)
  between operations  15.1 us (3%)
    transpose x2, matrix products, kernel_grad(): return jnp.transpose(result, (1, 0, 2, 3, 4))  135 us
    psum x1, blocking collectives, on_device(): lax.psum((grad_w_one, grad_b_one, grad_w_two, grad_b_two), 'space')  60 us
    psum x1, waiting for transfers between devices, on_device(): lax.psum((grad_w_one, grad_b_one, grad_w_two, grad_b_two), 'space')  50.4 us
    concatenate x4, other arithmetic, extend(): return widen_last(jnp.concatenate([low_y, wide, high_y], axis=2))  40.3 us
    ppermute x12, starting transfers between devices, from_behind(): lax.ppermute(value, axis, [(source, source + steps) for source in range(f...  37 us
    conv_general_dilated x3, matrix products, correlate(): lax.conv_general_dilated(padded, kernel, (1, 1, 1), 'VALID', dimension_nu...  28 us
    concatenate x5, local copies, waits for them, and re-layouts, extend(): return widen_last(jnp.concatenate([low_y, wide, high_y], axis=2))  26.5 us
    select_n x3, local copies, waits for them, and re-layouts, slope(): return jnp.where(pre > 0, 1.0, 0.3)  15.8 us
  transfers between devices with their start and end apart: 14, of which 1 were waited for; matrix products, arithmetic and copies ran while one was open for 61% of the time, Pallas kernels for 0%

profile of v1, /device:TPU:0, one launch (start us, length us, event | category | flops | bytes accessed | tf_op | source)
XLA Modules:
  0.0 484.9 jit_solution(7398800802604551089)
XLA Ops:
  13.0 5.2 %collective-permute-start.4 = (bf16[1,32,4,1,128]{4,1,3,2,0:T(8,128)(2,1)S(1)}, bf16[1,32,4,1,128]{4,1,3,2,0:T(8,128)(2,1)S(1)}, u32[]{:S(2)}, u32[]{:S(2)}) collective-permute-start(bf16[1,32,4,1,128]{4,1,3,2,0:T(8,128)(2,1)S(1)} %get-tuple-element.22), channel_id=1, source_target_pairs={{0,1},{1,2},{2,3},{3,4},{4,5},{5,6},{6,7},{7,8},{8,9},{9,10},{10,1... | collective-permute-start | bytes 98312 | tf_op jit(solution)/shard_map/ppermute | solution.py:12
  20.3 9.1 %copy.94 = bf16[1,4,8,8,256]{1,0,4,3,2:T(2,128)(2,1)} copy(bf16[1,4,8,8,256]{4,3,2,1,0:T(8,128)(2,1)S(1)} %dynamic-slice_bitcast_fusion) | data formatting | bytes 262144 | tf_op jit(solution)/shard_map/dynamic_slice | solution.py:103
  30.8 7.0 %pad_maximum_fusion.3 = (bf16[1,4,1,10,256]{1,0,4,3,2:T(2,128)(2,1)}, bf16[1,4,1,10,256]{1,0,4,3,2:T(2,128)(2,1)}) fusion(bf16[1,4,8,1,256]{1,0,4,3,2:T(2,128)(2,1)S(1)} %copy.95, bf16[1,4,8,8,256]{1,0,4,3,2:T(2,128)(2,1)} %copy.94, bf16[1,4,8,1,256]{1,0,4,3,2:T(2,128)(2,1)S(1)} %copy.93), kind=kLoop, calls=%fused_computation.43 | loop fusion | flops 40960 | bytes 204800 | tf_op jit(solution)/shard_map/slice | solution.py:73
  37.9 2.5 copy.96
  40.4 5.9 %collective-permute-start.2 = (bf16[1,4,1,10,256]{4,1,3,2,0:T(4,128)(2,1)S(1)}, bf16[1,4,1,10,256]{4,1,3,2,0:T(4,128)(2,1)S(1)}, u32[]{:S(2)}, u32[]{:S(2)}) collective-permute-start(bf16[1,4,1,10,256]{4,1,3,2,0:T(4,128)(2,1)S(1)} %copy.96), channel_id=1, source_target_pairs={{0,2},{1,3},{2,4},{3,5},{4,6},{5,7},{6,8},{7,9},{8,10},{9,11},{10,... | collective-permute-start | bytes 61448 | tf_op jit(solution)/shard_map/ppermute | solution.py:12
  46.3 2.5 copy.97
  50.1 5.9 %collective-permute-start.6 = (bf16[1,32,1,6,128]{4,1,3,2,0:T(8,128)(2,1)S(1)}, bf16[1,32,1,6,128]{4,1,3,2,0:T(8,128)(2,1)S(1)}, u32[]{:S(2)}, u32[]{:S(2)}) collective-permute-start(bf16[1,32,1,6,128]{4,1,3,2,0:T(8,128)(2,1)S(1)} %get-tuple-element.20), channel_id=1, source_target_pairs={{0,2},{1,3},{2,4},{3,5},{4,6},{5,7},{6,8},{7,9},{8,10},{9,11},{10,... | collective-permute-start | bytes 147464 | tf_op jit(solution)/shard_map/ppermute | solution.py:12
  61.8 40.1 %pad_maximum_fusion = bf16[1,4,10,10,256]{1,0,4,3,2:T(2,128)(2,1)} fusion(bf16[1,4,1,10,256]{1,0,4,3,2:T(2,128)(2,1)} %copy.99, bf16[1,4,8,1,256]{1,0,4,3,2:T(2,128)(2,1)S(1)} %copy.95, bf16[1,4,8,8,256]{1,0,4,3,2:T(2,128)(2,1)} %copy.94, bf16[1,4,8,1,256]{1,0,4,3,2:T(2,128)(2,1)S(1)} %copy.93, bf16[1,4,1,10,256]{1,0,4,3,2:T(2,128)(2,1)} %copy.98), kind=kLoop, calls=%fused_computation | loop fusion | flops 409600 | bytes 409600 | tf_op jit(solution)/shard_map/concatenate | solution.py:75
  101.9 23.7 %copy.113 = bf16[1,4,10,10,256]{4,1,3,2,0:T(4,128)(2,1)S(1)} copy(bf16[1,4,10,10,256]{1,0,4,3,2:T(2,128)(2,1)} %pad_maximum_fusion) | data formatting | bytes 409600 | tf_op jit(solution)/shard_map/concatenate | solution.py:75
  126.6 4.3 copy.115
  135.3 3.0 copy.103
  139.3 3.5 fusion.53
  151.2 23.9 %fusion.58 = f32[64,32,3,3,3]{0,1,4,3,2:T(8,128)} fusion(bf16[1,32,6,6,128]{1,0,4,3,2:T(2,128)(2,1)S(1)} %copy.119, bf16[1,64,4,4,128]{1,3,4,2,0:T(4,128)(2,1)S(1)} %get-tuple-element.11), kind=kOutput, calls=%fused_computation.50 | convolution fusion | flops 225312768 | bytes 778240 | tf_op jit(solution)/shard_map/transpose | solution.py:35
  177.7 7.7 %collective-permute-start.10 = (bf16[1,64,1,6,128]{4,1,3,2,0:T(8,128)(2,1)S(1)}, bf16[1,64,1,6,128]{4,1,3,2,0:T(8,128)(2,1)S(1)}, u32[]{:S(2)}, u32[]{:S(2)}) collective-permute-start(bf16[1,64,1,6,128]{4,1,3,2,0:T(8,128)(2,1)S(1)} %get-tuple-element.18), channel_id=1, source_target_pairs={{0,2},{1,3},{2,4},{3,5},{4,6},{5,7},{6,8},{7,9},{8,10},{9,11},{10,... | collective-permute-start | bytes 294920 | tf_op jit(solution)/shard_map/ppermute | solution.py:12
  186.8 20.2 %fusion = f32[8,8,8,33,32]{4,2,3,1,0:T(8,128)S(1)} fusion(f32[32]{0:T(128)S(1)} %copy-done.11, pred[8,33]{0,1:T(8,128)(4,1)S(1)} %copy-done.12, bf16[32,4,3,3,3]{0,1,4,3,2:T(4,128)(2,1)S(1)} %copy-done.9, bf16[4,10,10,1,7,2]{4,0,5,2,1,3:T(4,128)(2,1)S(1)} %copy-done.2, bf16[4,10,10,1,8,33]{4,0,5,2,1,3:T(4,128)(2,1)} %copy.115), kind=kOutput, calls=%fused_computation.2 | convolution fusion | flops 119619840 | bytes 2392392 | tf_op jit(solution)/shard_map/conv_general_dilated | solution.py:16
  207.0 6.0 %copy.121 = f32[8,8,8,33,32]{4,3,2,1,0:T(8,128)} copy(f32[8,8,8,33,32]{4,2,3,1,0:T(8,128)S(1)} %fusion) | data formatting | bytes 4325376 | tf_op jit(solution)/shard_map/jit(_where)/select_n | solution.py:52
  213.0 9.5 %reshape.76 = f32[8,8,1,264,32]{4,3,1,0,2:T(8,128)} reshape(f32[8,8,8,33,32]{4,3,2,1,0:T(8,128)} %copy.121) | data formatting | bytes 4325376 | tf_op jit(solution)/shard_map/jit(_where)/select_n | solution.py:52
  222.5 50.4 %all-reduce.5.cloned.1.call-done = f32[64,32,3,3,3]{0,1,4,3,2:T(8,128)} async-done(((f32[64,32,3,3,3]{0,1,4,3,2:T(8,128)}), f32[64,32,3,3,3]{0,1,4,3,2:T(8,128)}) %all-reduce.5.cloned.1.call-update) | async-done | bytes 221200 | tf_op jit(solution)/shard_map/psum | solution.py:114
  275.9 4.3 fusion.50
  280.7 7.3 %broadcast_in_dim.41 = f32[32,4,2,4,2,128,2]{0,6,5,4,3,2,1:T(2,128)} broadcast(f32[32,4,4,128]{0,3,2,1:T(8,128)S(1)} %copy.112), dimensions={0,1,3,5} | broadcast | bytes 2359296 | tf_op jit(solution)/shard_map/broadcast_in_dim | solution.py:45
  288.0 7.6 %convert_reduce_fusion = (f32[32]{0:T(128)}, bf16[1,32,8,8,256]{1,4,3,2,0:T(8,128)(2,1)S(1)}) fusion(f32[1,32,8,8,256]{1,4,3,2,0:T(8,128)} %bitcast.76, f32[8,8,1,264,32]{4,3,1,0,2:T(8,128)} %reshape.76), kind=kLoop, calls=%fused_computation.6 | loop fusion | flops 2097120 | bytes 5243008 | tf_op jit(solution)/shard_map/reduce_sum | solution.py:88
  295.6 111.0 %fusion.3 = f32[32,4,3,3,3]{0,1,4,3,2:T(4,128)S(1)} fusion(bf16[1,4,10,10,256]{1,0,4,3,2:T(2,128)(2,1)} %pad_maximum_fusion, bf16[1,32,8,8,256]{1,4,3,2,0:T(8,128)(2,1)S(1)} %get-tuple-element.13), kind=kOutput, calls=%fused_computation.7 | convolution fusion | flops 112951296 | bytes 1267200 | tf_op jit(solution)/shard_map/transpose | solution.py:35
  406.6 60.0 %all-reduce = (f32[32,4,3,3,3]{0,1,4,3,2:T(4,128)S(1)}, f32[32]{0:T(128)S(1)}, f32[64]{0:T(128)S(1)}) all-reduce(f32[32,4,3,3,3]{0,1,4,3,2:T(4,128)S(1)} %fusion.3, f32[32]{0:T(128)S(1)} %copy-done.5, f32[64]{0:T(128)S(1)} %copy-done.6), channel_id=1, replica_groups=mesh['section'=2,'space'=16] {'space'}, use_global_device_ids=true, to_apply=%region_0.1 | all-reduce | flops 3552 | bytes 28416 | tf_op jit(solution)/shard_map/psum | solution.py:114
  466.6 9.2 %all-reduce.1 = (f32[32,4,3,3,3]{0,1,4,3,2:T(4,128)}, f32[32]{0:T(128)}, f32[64]{0:T(128)}) all-reduce(f32[32,4,3,3,3]{0,1,4,3,2:T(4,128)S(1)} %get-tuple-element.4, f32[32]{0:T(128)S(1)} %get-tuple-element.5, f32[64]{0:T(128)S(1)} %get-tuple-element.6), channel_id=1, replica_groups=mesh['section'=2,'space'=16] {'section'}, use_global_device_ids=true, to_apply=%region_1.2 | all-reduce | flops 3552 | bytes 28416 | tf_op jit(solution)/shard_map/psum | solution.py:115
  (96 shorter events, 40.0 us)
Async XLA Ops:
  7.2 265.8 %all-reduce.5.cloned.1.call-start = ((), (), s32[]{:S(2)}) async-start(), calls=%async_computation | async-start | bytes 884736 | tf_op jit(solution)/shard_map/psum | solution.py:114
  8.2 21.3 %collective-permute-start = (bf16[1,4,8,1,256]{4,2,3,1,0:T(8,128)(2,1)S(1)}, bf16[1,4,8,1,256]{4,2,3,1,0:T(8,128)(2,1)S(1)}, u32[]{:S(2)}, u32[]{:S(2)}) collective-permute-start(bf16[1,4,8,1,256]{4,2,3,1,0:T(8,128)(2,1)S(1)} %copy.91), channel_id=1, source_target_pairs={{0,1},{1,2},{2,3},{3,4},{4,5},{5,6},{6,7},{7,8},{8,9},{9,10},{10,1... | collective-permute-start | bytes 49160 | tf_op jit(solution)/shard_map/ppermute | solution.py:12
  10.7 19.5 %collective-permute-start.1 = (bf16[1,4,8,1,256]{4,2,3,1,0:T(8,128)(2,1)S(1)}, bf16[1,4,8,1,256]{4,2,3,1,0:T(8,128)(2,1)S(1)}, u32[]{:S(2)}, u32[]{:S(2)}) collective-permute-start(bf16[1,4,8,1,256]{4,2,3,1,0:T(8,128)(2,1)S(1)} %copy.92), channel_id=1, source_target_pairs={{1,0},{2,1},{3,2},{4,3},{5,4},{6,5},{7,6},{8,7},{9,8},{10,9},{11,1... | collective-permute-start | bytes 49160 | tf_op jit(solution)/shard_map/ppermute | solution.py:12
  13.0 37.1 %collective-permute-start.4 = (bf16[1,32,4,1,128]{4,1,3,2,0:T(8,128)(2,1)S(1)}, bf16[1,32,4,1,128]{4,1,3,2,0:T(8,128)(2,1)S(1)}, u32[]{:S(2)}, u32[]{:S(2)}) collective-permute-start(bf16[1,32,4,1,128]{4,1,3,2,0:T(8,128)(2,1)S(1)} %get-tuple-element.22), channel_id=1, source_target_pairs={{0,1},{1,2},{2,3},{3,4},{4,5},{5,6},{6,7},{7,8},{8,9},{9,10},{10,1... | collective-permute-start | bytes 98312 | tf_op jit(solution)/shard_map/ppermute | solution.py:12
  18.1 32.0 %collective-permute-start.5 = (bf16[1,32,4,1,128]{4,1,3,2,0:T(8,128)(2,1)S(1)}, bf16[1,32,4,1,128]{4,1,3,2,0:T(8,128)(2,1)S(1)}, u32[]{:S(2)}, u32[]{:S(2)}) collective-permute-start(bf16[1,32,4,1,128]{4,1,3,2,0:T(8,128)(2,1)S(1)} %get-tuple-element.23), channel_id=1, source_target_pairs={{1,0},{2,1},{3,2},{4,3},{5,4},{6,5},{7,6},{8,7},{9,8},{10,9},{11,1... | collective-permute-start | bytes 98312 | tf_op jit(solution)/shard_map/ppermute | solution.py:12
  40.4 17.1 %collective-permute-start.2 = (bf16[1,4,1,10,256]{4,1,3,2,0:T(4,128)(2,1)S(1)}, bf16[1,4,1,10,256]{4,1,3,2,0:T(4,128)(2,1)S(1)}, u32[]{:S(2)}, u32[]{:S(2)}) collective-permute-start(bf16[1,4,1,10,256]{4,1,3,2,0:T(4,128)(2,1)S(1)} %copy.96), channel_id=1, source_target_pairs={{0,2},{1,3},{2,4},{3,5},{4,6},{5,7},{6,8},{7,9},{8,10},{9,11},{10,... | collective-permute-start | bytes 61448 | tf_op jit(solution)/shard_map/ppermute | solution.py:12
  48.8 10.9 %collective-permute-start.3 = (bf16[1,4,1,10,256]{4,1,3,2,0:T(4,128)(2,1)S(1)}, bf16[1,4,1,10,256]{4,1,3,2,0:T(4,128)(2,1)S(1)}, u32[]{:S(2)}, u32[]{:S(2)}) collective-permute-start(bf16[1,4,1,10,256]{4,1,3,2,0:T(4,128)(2,1)S(1)} %copy.97), channel_id=1, source_target_pairs={{2,0},{3,1},{4,2},{5,3},{6,4},{7,5},{8,6},{9,7},{10,8},{11,9},{12,... | collective-permute-start | bytes 61448 | tf_op jit(solution)/shard_map/ppermute | solution.py:12
  50.1 82.6 %collective-permute-start.6 = (bf16[1,32,1,6,128]{4,1,3,2,0:T(8,128)(2,1)S(1)}, bf16[1,32,1,6,128]{4,1,3,2,0:T(8,128)(2,1)S(1)}, u32[]{:S(2)}, u32[]{:S(2)}) collective-permute-start(bf16[1,32,1,6,128]{4,1,3,2,0:T(8,128)(2,1)S(1)} %get-tuple-element.20), channel_id=1, source_target_pairs={{0,2},{1,3},{2,4},{3,5},{4,6},{5,7},{6,8},{7,9},{8,10},{9,11},{10,... | collective-permute-start | bytes 147464 | tf_op jit(solution)/shard_map/ppermute | solution.py:12
  56.0 76.7 %collective-permute-start.7 = (bf16[1,32,1,6,128]{4,1,3,2,0:T(8,128)(2,1)S(1)}, bf16[1,32,1,6,128]{4,1,3,2,0:T(8,128)(2,1)S(1)}, u32[]{:S(2)}, u32[]{:S(2)}) collective-permute-start(bf16[1,32,1,6,128]{4,1,3,2,0:T(8,128)(2,1)S(1)} %get-tuple-element.21), channel_id=1, source_target_pairs={{2,0},{3,1},{4,2},{5,3},{6,4},{7,5},{8,6},{9,7},{10,8},{11,9},{12,... | collective-permute-start | bytes 147464 | tf_op jit(solution)/shard_map/ppermute | solution.py:12
  135.3 4.0 copy-start.7
  135.3 4.0 copy-start.10
  143.1 6.1 %copy-start.4 = (bf16[1,32,1,6,128]{4,1,3,2,0:T(8,128)(2,1)S(1)}, bf16[1,32,1,6,128]{4,1,3,2,0:T(8,128)(2,1)}, u32[]{:S(2)}) copy-start(bf16[1,32,1,6,128]{4,1,3,2,0:T(8,128)(2,1)} %copy-done.3) | copy-start | bytes 147460
  145.9 29.6 %collective-permute-start.8 = (bf16[1,64,4,1,128]{1,3,4,2,0:T(2,128)(2,1)}, bf16[1,64,4,1,128]{1,3,4,2,0:T(2,128)(2,1)}, u32[]{:S(2)}, u32[]{:S(2)}) collective-permute-start(bf16[1,64,4,1,128]{1,3,4,2,0:T(2,128)(2,1)} %get-tuple-element.16), channel_id=1, source_target_pairs={{0,1},{1,2},{2,3},{3,4},{4,5},{5,6},{6,7},{7,8},{8,9},{9,10},{10,1... | collective-permute-start | bytes 196616 | tf_op jit(solution)/shard_map/ppermute | solution.py:12
  147.9 28.7 %collective-permute-start.9 = (bf16[1,64,4,1,128]{1,3,4,2,0:T(2,128)(2,1)}, bf16[1,64,4,1,128]{1,3,4,2,0:T(2,128)(2,1)}, u32[]{:S(2)}, u32[]{:S(2)}) collective-permute-start(bf16[1,64,4,1,128]{1,3,4,2,0:T(2,128)(2,1)} %get-tuple-element.17), channel_id=1, source_target_pairs={{1,0},{2,1},{3,2},{4,3},{5,4},{6,5},{7,6},{8,7},{9,8},{10,9},{11,1... | collective-permute-start | bytes 196616 | tf_op jit(solution)/shard_map/ppermute | solution.py:12
  175.1 11.6 %copy-start.2 = (bf16[4,10,10,1,7,2]{4,0,5,2,1,3:T(4,128)(2,1)S(1)}, bf16[4,10,10,1,7,2]{4,0,5,2,1,3:T(4,128)(2,1)}, u32[]{:S(2)}) copy-start(bf16[4,10,10,1,7,2]{4,0,5,2,1,3:T(4,128)(2,1)} %slice.64) | copy-start | bytes 33604
  175.2 11.6 %copy-start.9 = (bf16[32,4,3,3,3]{0,1,4,3,2:T(4,128)(2,1)S(1)}, bf16[32,4,3,3,3]{0,1,4,3,2:T(4,128)(2,1)}, u32[]{:S(2)}) copy-start(bf16[32,4,3,3,3]{0,1,4,3,2:T(4,128)(2,1)} %param.10) | copy-start | bytes 20740
  175.2 11.6 %copy-start.11 = (f32[32]{0:T(128)S(1)}, f32[32]{0:T(128)}, u32[]{:S(2)}) copy-start(f32[32]{0:T(128)} %param.11) | copy-start | bytes 388
  175.2 11.6 %copy-start.12 = (pred[8,33]{0,1:T(8,128)(4,1)S(1)}, pred[8,33]{0,1:T(8,128)(4,1)}, u32[]{:S(2)}) copy-start(pred[8,33]{0,1:T(8,128)(4,1)} %constant.64) | copy-start | bytes 796
  175.5 300.4 %all-reduce.7.cloned.1.call-start = ((), (), s32[]{:S(2)}) async-start(), calls=%async_computation.1 | async-start | bytes 884736 | tf_op jit(solution)/shard_map/psum | solution.py:115
  177.7 95.3 %collective-permute-start.10 = (bf16[1,64,1,6,128]{4,1,3,2,0:T(8,128)(2,1)S(1)}, bf16[1,64,1,6,128]{4,1,3,2,0:T(8,128)(2,1)S(1)}, u32[]{:S(2)}, u32[]{:S(2)}) collective-permute-start(bf16[1,64,1,6,128]{4,1,3,2,0:T(8,128)(2,1)S(1)} %get-tuple-element.18), channel_id=1, source_target_pairs={{0,2},{1,3},{2,4},{3,5},{4,6},{5,7},{6,8},{7,9},{8,10},{9,11},{10,... | collective-permute-start | bytes 294920 | tf_op jit(solution)/shard_map/ppermute | solution.py:12
  185.5 87.5 %collective-permute-start.11 = (bf16[1,64,1,6,128]{4,1,3,2,0:T(8,128)(2,1)S(1)}, bf16[1,64,1,6,128]{4,1,3,2,0:T(8,128)(2,1)S(1)}, u32[]{:S(2)}, u32[]{:S(2)}) collective-permute-start(bf16[1,64,1,6,128]{4,1,3,2,0:T(8,128)(2,1)S(1)} %get-tuple-element.19), channel_id=1, source_target_pairs={{2,0},{3,1},{4,2},{5,3},{6,4},{7,5},{8,6},{9,7},{10,8},{11,9},{12,... | collective-permute-start | bytes 294920 | tf_op jit(solution)/shard_map/ppermute | solution.py:12
  295.6 111.0 %copy-start.5 = (f32[32]{0:T(128)S(1)}, f32[32]{0:T(128)}, u32[]{:S(2)}) copy-start(f32[32]{0:T(128)} %get-tuple-element.12) | copy-start | bytes 388
  295.6 111.0 %copy-start.6 = (f32[64]{0:T(128)S(1)}, f32[64]{0:T(128)}, u32[]{:S(2)}) copy-start(f32[64]{0:T(128)} %get-tuple-element.10) | copy-start | bytes 772
  295.6 182.0 %copy-start.1 = (bf16[1,2,4,8,8,256]{5,4,3,2,1,0:T(8,128)(2,1)S(1)}, bf16[1,2,4,8,8,256]{5,4,3,2,1,0:T(8,128)(2,1)}, u32[]{:S(2)}) copy-start(bf16[1,2,4,8,8,256]{5,4,3,2,1,0:T(8,128)(2,1)} %param.7) | copy-start | bytes 786436
  (5 other events, 7.4 us)
Sparse Core Ops, SparseCore 0:
  175.6 97.3 all-reduce.4
  275.2 27.2 all-reduce.6
